TPU v7x, 32 devices: a whole 2x2x4 slice. The times are simulated.
32 devices in a mesh: runs: 2 (over y), gx: 4 (over z), gy: 2 (over core), gz: 2 (over x).
Axes of the slice: x: 2, y: 2, z: 4, core: 2. Of those that a mesh axis runs over, the one named last changes fastest.
Arguments:
- labels: int32 [24, 128, 1024], P(('runs', 'gz'), 'gx', 'gy'), parts along dimension 0, may hold values from 0 to 3
- background: bfloat16 [24, 128, 1024], P(('runs', 'gz'), 'gx', 'gy'), parts along dimension 0, may hold values from -3 to 3
- contrasts: float32 [8], P('runs'), parts along dimension 0, may hold values from -1 to 1
- kernels: bfloat16 [24, 15, 15], P(('runs', 'gz')), parts along dimension 0, may hold values from -0.125 to 0.125
- observed: float32 [6, 128, 1024], P('runs', 'gx', 'gy'), parts along dimension 0, may hold values from -6 to 6
Outputs:
- residual: float32 [6, 128, 1024], P('runs', ('gx', 'gz'), 'gy'), parts along dimension 0
- gradient: float32 [24, 128, 1024], P(('runs', 'gz'), 'gx', 'gy'), parts along dimension 0
There are 2 independent parts, one for each index of `runs`. A program takes and returns all parts, laid end to end along the dimension named above; each array names one. Nothing has to cross between parts.
All inputs are finite; a program needn't handle non-finite values.
Results may differ from a plain program's by a relative error of at most 0.0058.
Values may be sent and summed in bfloat16 or wider, within the bound.
No kernel may reach another device: no remote copies, remote signals or barrier semaphores. Data moves between devices by JAX's collectives and lax.ppermute only.
A program may use at most 64 MiB of HBM per device.

v0:
```python
import jax
import jax.numpy as jnp
from jax import lax
from jax.sharding import PartitionSpec as P

ITERS = 2
descent = 0.01


def padded_2(value, sides, width):
    for axis, dim in sides:
        peers, length = (lax.axis_size(axis), value.shape[dim])
        up = [(i, (i + 1) % peers) for i in range(peers)]
        down = [(j, i) for i, j in up]
        last = lax.slice_in_dim(value, length - width, length, axis=dim)
        initial = lax.slice_in_dim(value, 0, width, axis=dim)
        before = lax.ppermute(last, axis, up)
        after = lax.ppermute(initial, axis, down)
        value = jnp.concatenate([before, value, after], axis=dim)
    return value


def band_selector(span, block_width):
    shape = (span, 2 * block_width, block_width)
    offset = lax.broadcasted_iota(jnp.int32, shape, 1) - lax.broadcasted_iota(jnp.int32, shape, 2)
    return jnp.where(offset == lax.broadcasted_iota(jnp.int32, shape, 0), 1.0, 0.0).astype(
        jnp.bfloat16
    )


def band_matrices(kernel, selector):
    summed = jnp.einsum("sc,cpq->spq", kernel, selector, preferred_element_type=jnp.float32)
    return summed.astype(jnp.bfloat16)


def banded_sum(padded, band_rows, row_count, blocks, block_width):
    pieces = []
    for row_shift in range(band_rows.shape[0]):
        window = padded[row_shift : row_shift + row_count]
        pieces.append(window[:, : blocks * block_width].reshape(row_count, blocks, block_width))
        pieces.append(
            window[:, block_width : (blocks + 1) * block_width].reshape(
                row_count, blocks, block_width
            )
        )
    stacked = jnp.concatenate(pieces, axis=2)
    weights = band_rows.reshape(band_rows.shape[0] * 2 * block_width, block_width)
    summed = jnp.einsum("rbk,kq->rbq", stacked, weights, preferred_element_type=jnp.float32)
    return summed.reshape(row_count, blocks * block_width)


def surface_halo(rounded, kernels, selector, block_width, blocks, radius):
    depth_count, cells_x, cells_y = rounded.shape
    padded = padded_2(rounded, (("gx", 1), ("gy", 2)), radius)
    padded = jnp.pad(padded, ((0, 0), (0, 0), (0, block_width - 2 * radius)))

    def add_layer(depth_index, summed):
        band_rows = band_matrices(
            lax.dynamic_index_in_dim(kernels, depth_index, 0, keepdims=False), selector
        )
        layer_cells = lax.dynamic_index_in_dim(padded, depth_index, 0, keepdims=False)
        return summed + banded_sum(layer_cells, band_rows, cells_x, blocks, block_width)

    return lax.fori_loop(0, depth_count, add_layer, jnp.zeros((cells_x, cells_y), jnp.float32))


def tensor_parts(edged_values):
    centre = edged_values[..., 1:-1, 1:-1]
    along_x = edged_values[..., 2:, 1:-1] + edged_values[..., :-2, 1:-1] - 2.0 * centre
    along_y = edged_values[..., 1:-1, 2:] + edged_values[..., 1:-1, :-2] - 2.0 * centre
    mixed = 0.25 * (
        edged_values[..., 2:, 2:]
        - edged_values[..., 2:, :-2]
        - edged_values[..., :-2, 2:]
        + edged_values[..., :-2, :-2]
    )
    return (along_x, along_y, mixed)


def adjoint_sum(edged_misfit):
    return (
        tensor_parts(edged_misfit[0])[0]
        + tensor_parts(edged_misfit[1])[1]
        + tensor_parts(edged_misfit[2])[2]
    )


def layer_gradients(adjoint_field, flipped, selector, block_width, blocks, radius):
    depth_count = flipped.shape[0]
    cells_x, cells_y = adjoint_field.shape
    padded = padded_2(adjoint_field, (("gx", 0), ("gy", 1)), radius)
    padded = jnp.pad(padded, ((0, 0), (0, block_width - 2 * radius)))

    def one_layer(depth_index, stacked):
        band_rows = band_matrices(
            lax.dynamic_index_in_dim(flipped, depth_index, 0, keepdims=False), selector
        )
        layer_grad = banded_sum(padded, band_rows, cells_x, blocks, block_width)
        return lax.dynamic_update_index_in_dim(stacked, layer_grad, depth_index, 0)

    return lax.fori_loop(
        0, depth_count, one_layer, jnp.zeros((depth_count, cells_x, cells_y), jnp.float32)
    )


def body(labels, background, contrasts, kernels, observed):
    cells_x = labels.shape[1]
    cells_y = labels.shape[2]
    block_width = min(cells_y, 128)
    blocks = cells_y // block_width
    radius = (kernels.shape[1] - 1) // 2
    share_rows = cells_x // lax.axis_size("gz")
    selector = band_selector(kernels.shape[2], block_width)
    flipped = kernels[:, ::-1, ::-1]
    density = background.astype(jnp.float32)
    for class_id in range(contrasts.shape[0]):
        density = density + jnp.where(labels == class_id, contrasts[class_id], 0.0)
    residual = observed[:, :share_rows]
    gradient = density
    for iteration in range(ITERS):
        rounded = density.astype(jnp.bfloat16)
        partial_value = surface_halo(rounded, kernels, selector, block_width, blocks, radius)
        surface = lax.psum(partial_value, "gz")
        edged_surface = padded_2(surface, (("gx", 0), ("gy", 1)), 1)
        misfit = jnp.stack(tensor_parts(edged_surface)) - observed
        edged_misfit = padded_2(misfit, (("gx", 1), ("gy", 2)), 1)
        adjoint_field = adjoint_sum(edged_misfit).astype(jnp.bfloat16)
        residual = lax.dynamic_slice_in_dim(
            misfit, lax.axis_index("gz") * share_rows, share_rows, 1
        )
        gradient = layer_gradients(adjoint_field, flipped, selector, block_width, blocks, radius)
        density = density - descent * gradient
    return (residual, gradient)


def solution(mesh):
    placed = (
        P(("runs", "gz"), "gx", "gy"),
        P(("runs", "gz"), "gx", "gy"),
        P("runs"),
        P(("runs", "gz"), None, None),
        P("runs", "gx", "gy"),
    )
    return jax.shard_map(
        body,
        mesh=mesh,
        in_specs=placed,
        out_specs=(P("runs", ("gx", "gz"), "gy"), P(("runs", "gz"), "gx", "gy")),
        check_vma=False,
    )
```

profile of v0, /device:TPU:0, one launch (start us, length us, event | category | flops | bytes accessed | tf_op | source)
XLA Modules:
  0.0 187.0 jit_solution(16644792273264350666)
XLA Ops:
  7.2 1.4 fusion.107
  8.6 3.6 %fusion.98 = bf16[6,32,512]{2,1,0:T(8,128)(2,1)S(1)} fusion(f32[]{:T(128)} %bitcast.3, s32[6,32,512]{2,1,0:T(8,128)} %param.13, f32[]{:T(128)} %bitcast.2, f32[]{:T(128)} %bitcast.1, f32[]{:T(128)} %bitcast, bf16[6,32,512]{2,1,0:T(8,128)(2,1)} %param.14), kind=kLoop, calls=%fused_computation.448 | loop fusion | flops 1376256 | bytes 786448 | tf_op jit(solution)/shard_map/convert_element_type | solution.py:121
  12.2 3.1 %collective-permute-start = (bf16[6,7,512]{2,1,0:T(8,128)(2,1)S(1)}, bf16[6,7,512]{2,1,0:T(8,128)(2,1)S(1)}, u32[]{:S(2)}, u32[]{:S(2)}) collective-permute-start(bf16[6,7,512]{2,1,0:T(8,128)(2,1)S(1)} %get-tuple-element.678), channel_id=1, source_target_pairs={{0,4},{4,8},{8,12},{12,0},{1,5},{5,9},{9,13},{13,1},{2,6},{6,10},{... | collective-permute-start | bytes 129032 | tf_op jit(solution)/shard_map/ppermute | solution.py:17
  15.3 2.1 %collective-permute-start.1 = (bf16[6,7,512]{2,1,0:T(8,128)(2,1)S(1)}, bf16[6,7,512]{2,1,0:T(8,128)(2,1)S(1)}, u32[]{:S(2)}, u32[]{:S(2)}) collective-permute-start(bf16[6,7,512]{2,1,0:T(8,128)(2,1)S(1)} %get-tuple-element.679), channel_id=1, source_target_pairs={{4,0},{8,4},{12,8},{0,12},{5,1},{9,5},{13,9},{1,13},{6,2},{10,6},{... | collective-permute-start | bytes 129032 | tf_op jit(solution)/shard_map/ppermute | solution.py:18
  17.4 2.1 %collective-permute-done = bf16[6,7,512]{2,1,0:T(8,128)(2,1)S(1)} collective-permute-done((bf16[6,7,512]{2,1,0:T(8,128)(2,1)S(1)}, bf16[6,7,512]{2,1,0:T(8,128)(2,1)S(1)}, u32[]{:S(2)}, u32[]{:S(2)}) %collective-permute-start) | collective-permute-done | bytes 43040 | tf_op jit(solution)/shard_map/ppermute | solution.py:17
  20.2 0.5 collective-permute-start.3
  20.7 0.8 collective-permute-done.2
  21.9 13.9 %while.62 = (s32[]{:T(128)}, f32[32,512]{1,0:T(8,128)S(1)}, bf16[6,46,640]{2,1,0:T(8,128)(2,1)S(1)}, bf16[6,15,15]{2,1,0:T(8,128)(2,1)S(1)}, s32[]{:T(128)}, /*i...) while((s32[]{:T(128)}, f32[32,512]{1,0:T(8,128)S(1)}, ...), condition=%wide.region_1.2_spmd.clone, body=%wide.region_0.1_spmd.clone.sunk | while | flops 143065104 | bytes 10342823 | solution.py:64
  23.1 0.4 convolution_convert_fusion.10
  25.4 0.4 convolution_convert_fusion.10
  30.0 0.4 convolution_convert_fusion.10
  32.4 0.4 convolution_convert_fusion.10
  35.9 0.6 copy-done
  36.6 22.2 %all-reduce.7.cloned.1.call-done = f32[32,512]{1,0:T(8,128)} async-done(((f32[32,512]{1,0:T(8,128)}), f32[32,512]{1,0:T(8,128)}) %all-reduce.7.cloned.1.call-update) | async-done | bytes 65552 | tf_op jit(solution)/shard_map/psum | solution.py:123
  58.8 0.7 fusion.104
  59.5 3.3 %collective-permute-start.4 = (f32[1,512]{1,0:T(1,128)S(1)}, f32[1,512]{1,0:T(1,128)S(1)}, u32[]{:S(2)}, u32[]{:S(2)}) collective-permute-start(f32[1,512]{1,0:T(1,128)S(1)} %get-tuple-element.693), channel_id=1, source_target_pairs={{4,0},{8,4},{12,8},{0,12},{5,1},{9,5},{13,9},{1,13},{6,2},{10,6},{... | collective-permute-start | bytes 6152 | tf_op jit(solution)/shard_map/ppermute | solution.py:18
  62.8 1.3 collective-permute-done.4
  64.1 4.1 %collective-permute-done.5 = f32[1,512]{1,0:T(1,128)S(1)} collective-permute-done((f32[1,512]{1,0:T(1,128)S(1)}, f32[1,512]{1,0:T(1,128)S(1)}, u32[]{:S(2)}, u32[]{:S(2)}) %collective-permute-start.5) | collective-permute-done | bytes 2080 | tf_op jit(solution)/shard_map/ppermute | solution.py:17
  68.2 0.8 pad_maximum_fusion.25
  69.1 0.5 collective-permute-start.7
  69.6 0.7 collective-permute-done.6
  70.4 1.0 pad_maximum_fusion.2
  71.4 1.1 fusion.86
  72.6 3.8 %collective-permute-start.9 = (f32[3,1,512]{2,1,0:T(1,128)S(1)}, f32[3,1,512]{2,1,0:T(1,128)S(1)}, u32[]{:S(2)}, u32[]{:S(2)}) collective-permute-start(f32[3,1,512]{2,1,0:T(1,128)S(1)} %get-tuple-element.677), channel_id=1, source_target_pairs={{4,0},{8,4},{12,8},{0,12},{5,1},{9,5},{13,9},{1,13},{6,2},{10,6},{... | collective-permute-start | bytes 18440 | tf_op jit(solution)/shard_map/ppermute | solution.py:18
  76.4 1.6 collective-permute-done.8
  78.2 0.5 collective-permute-start.11
  78.7 0.7 collective-permute-done.10
  80.1 3.9 %collective-permute-start.13 = (bf16[7,512]{1,0:T(8,128)(2,1)S(1)}, bf16[7,512]{1,0:T(8,128)(2,1)S(1)}, u32[]{:S(2)}, u32[]{:S(2)}) collective-permute-start(bf16[7,512]{1,0:T(8,128)(2,1)S(1)} %get-tuple-element.761), channel_id=1, source_target_pairs={{4,0},{8,4},{12,8},{0,12},{5,1},{9,5},{13,9},{1,13},{6,2},{10,6},{... | collective-permute-start | bytes 21512 | tf_op jit(solution)/shard_map/ppermute | solution.py:18
  84.0 1.6 collective-permute-done.12
  85.7 0.5 collective-permute-start.15
  86.3 0.6 collective-permute-done.14
  88.1 7.6 %while.60 = (s32[]{:T(128)}, f32[6,32,512]{2,1,0:T(8,128)S(1)}, bf16[6,15,15]{2,1,0:T(8,128)(2,1)S(1)}, bf16[32,4,3840]{2,0,1:T(8,128)(2,1)S(1)}, s32[]{:T(128)}) while((s32[]{:T(128)}, f32[6,32,512]{2,1,0:T(8,128)S(1)}, bf16[6,15,15]{2,1,0:T(8,128)(2,1)S(1)}, bf16[32,4,3840]{2,0,1:T(8,128)(2,1)S(1)}, s32[]{:T(128)}) %tuple.339), condition=%wide.region_4.5_spmd.clone, body=%wide.region_3.4_spmd.clone.sunk | while | flops 143032320 | bytes 5378117 | solution.py:101
  95.7 2.6 %subtract_convert_fusion = bf16[6,32,512]{2,1,0:T(8,128)(2,1)S(1)} fusion(f32[6,32,512]{2,1,0:T(8,128)S(1)} %get-tuple-element.447, f32[]{:T(128)} %bitcast.3, s32[6,32,512]{2,1,0:T(8,128)S(1)} %copy-done.2, f32[]{:T(128)} %bitcast.2, f32[]{:T(128)} %bitcast.1, f32[]{:T(128)} %bitcast, bf16[6,32,512]{2,1,0:T(8,128)(2,1)S(1)} %copy-done.3), kind=kLoop, calls=%fused_computation.213 | loop fusion | flops 1572864 | bytes 1179664 | tf_op jit(solution)/shard_map/convert_element_type | solution.py:121
  98.3 1.1 collective-permute-start.16
  99.5 2.8 %collective-permute-start.17 = (bf16[6,7,512]{2,1,0:T(8,128)(2,1)S(1)}, bf16[6,7,512]{2,1,0:T(8,128)(2,1)S(1)}, u32[]{:S(2)}, u32[]{:S(2)}) collective-permute-start(bf16[6,7,512]{2,1,0:T(8,128)(2,1)S(1)} %get-tuple-element.675), channel_id=1, source_target_pairs={{4,0},{8,4},{12,8},{0,12},{5,1},{9,5},{13,9},{1,13},{6,2},{10,6},{... | collective-permute-start | bytes 129032 | tf_op jit(solution)/shard_map/ppermute | solution.py:18
  102.3 2.3 %collective-permute-done.16 = bf16[6,7,512]{2,1,0:T(8,128)(2,1)S(1)} collective-permute-done((bf16[6,7,512]{2,1,0:T(8,128)(2,1)S(1)}, bf16[6,7,512]{2,1,0:T(8,128)(2,1)S(1)}, u32[]{:S(2)}, u32[]{:S(2)}) %collective-permute-start.16) | collective-permute-done | bytes 43040 | tf_op jit(solution)/shard_map/ppermute | solution.py:17
  104.8 0.5 collective-permute-start.19
  105.3 0.8 collective-permute-done.18
  106.5 14.0 %while.63 = (s32[]{:T(128)}, f32[32,512]{1,0:T(8,128)S(1)}, bf16[6,46,640]{2,1,0:T(8,128)(2,1)S(1)}, bf16[6,15,15]{2,1,0:T(8,128)(2,1)S(1)}, s32[]{:T(128)}, /*i...) while((s32[]{:T(128)}, f32[32,512]{1,0:T(8,128)S(1)}, ...), condition=%wide.region_6.7_spmd.clone, body=%wide.region_5.6_spmd.clone.sunk | while | flops 143065104 | bytes 10342823 | solution.py:64
  110.0 0.4 convolution_convert_fusion.11
  112.3 0.4 convolution_convert_fusion.11
  114.7 0.4 convolution_convert_fusion.11
  117.0 0.4 convolution_convert_fusion.11
  120.5 0.6 copy-done.1
  121.2 21.3 %all-reduce.9.cloned.1.call-done = f32[32,512]{1,0:T(8,128)} async-done(((f32[32,512]{1,0:T(8,128)}), f32[32,512]{1,0:T(8,128)}) %all-reduce.9.cloned.1.call-update) | async-done | bytes 65552 | tf_op jit(solution)/shard_map/psum | solution.py:123
  142.5 0.7 fusion.103
  143.2 3.3 %collective-permute-start.20 = (f32[1,512]{1,0:T(1,128)S(1)}, f32[1,512]{1,0:T(1,128)S(1)}, u32[]{:S(2)}, u32[]{:S(2)}) collective-permute-start(f32[1,512]{1,0:T(1,128)S(1)} %get-tuple-element.690), channel_id=1, source_target_pairs={{4,0},{8,4},{12,8},{0,12},{5,1},{9,5},{13,9},{1,13},{6,2},{10,6},{... | collective-permute-start | bytes 6152 | tf_op jit(solution)/shard_map/ppermute | solution.py:18
  146.6 1.3 collective-permute-done.20
  147.9 4.1 %collective-permute-done.21 = f32[1,512]{1,0:T(1,128)S(1)} collective-permute-done((f32[1,512]{1,0:T(1,128)S(1)}, f32[1,512]{1,0:T(1,128)S(1)}, u32[]{:S(2)}, u32[]{:S(2)}) %collective-permute-start.21) | collective-permute-done | bytes 2080 | tf_op jit(solution)/shard_map/ppermute | solution.py:17
  151.9 0.8 pad_maximum_fusion.22
  152.8 0.5 collective-permute-start.23
  153.3 0.7 collective-permute-done.22
  154.1 1.0 pad_maximum_fusion.3
  155.1 1.1 fusion.73
  156.3 3.8 %collective-permute-start.25 = (f32[3,1,512]{2,1,0:T(1,128)S(1)}, f32[3,1,512]{2,1,0:T(1,128)S(1)}, u32[]{:S(2)}, u32[]{:S(2)}) collective-permute-start(f32[3,1,512]{2,1,0:T(1,128)S(1)} %get-tuple-element.673), channel_id=1, source_target_pairs={{4,0},{8,4},{12,8},{0,12},{5,1},{9,5},{13,9},{1,13},{6,2},{10,6},{... | collective-permute-start | bytes 18440 | tf_op jit(solution)/shard_map/ppermute | solution.py:18
  160.1 1.6 collective-permute-done.24
  161.9 0.5 collective-permute-start.27
  162.4 0.7 collective-permute-done.26
  163.8 3.9 %collective-permute-start.29 = (bf16[7,512]{1,0:T(8,128)(2,1)S(1)}, bf16[7,512]{1,0:T(8,128)(2,1)S(1)}, u32[]{:S(2)}, u32[]{:S(2)}) collective-permute-start(bf16[7,512]{1,0:T(8,128)(2,1)S(1)} %get-tuple-element.759), channel_id=1, source_target_pairs={{4,0},{8,4},{12,8},{0,12},{5,1},{9,5},{13,9},{1,13},{6,2},{10,6},{... | collective-permute-start | bytes 21512 | tf_op jit(solution)/shard_map/ppermute | solution.py:18
  167.7 1.6 collective-permute-done.28
  169.4 0.5 collective-permute-start.31
  169.9 0.6 constant_dynamic-slice_fusion
  171.8 7.6 %while.61 = (s32[]{:T(128)}, f32[6,32,512]{2,1,0:T(8,128)S(1)}, bf16[6,15,15]{2,1,0:T(8,128)(2,1)S(1)}, bf16[32,4,3840]{2,0,1:T(8,128)(2,1)S(1)}, s32[]{:T(128)}) while((s32[]{:T(128)}, f32[6,32,512]{2,1,0:T(8,128)S(1)}, bf16[6,15,15]{2,1,0:T(8,128)(2,1)S(1)}, bf16[32,4,3840]{2,0,1:T(8,128)(2,1)S(1)}, s32[]{:T(128)}) %tuple.354), condition=%wide.region_9.10_spmd.clone, body=%wide.region_8.9_spmd.clone.sunk | while | flops 143032320 | bytes 5378117 | solution.py:101
  179.4 0.7 copy-done.5
  (719 shorter events, 41.4 us)
Async XLA Ops:
  7.2 51.6 %all-reduce.7.cloned.1.call-start = ((), (), s32[]{:S(2)}) async-start(), calls=%async_computation | async-start | bytes 131072 | tf_op jit(solution)/shard_map/psum | solution.py:123
  8.6 13.3 %copy-start.6 = (bf16[6,15,15]{2,1,0:T(8,128)(2,1)S(1)}, bf16[6,15,15]{2,1,0:T(8,128)(2,1)}, u32[]{:S(2)}) copy-start(bf16[6,15,15]{2,1,0:T(8,128)(2,1)} %param.16) | copy-start | bytes 8104
  12.2 7.3 %collective-permute-start = (bf16[6,7,512]{2,1,0:T(8,128)(2,1)S(1)}, bf16[6,7,512]{2,1,0:T(8,128)(2,1)S(1)}, u32[]{:S(2)}, u32[]{:S(2)}) collective-permute-start(bf16[6,7,512]{2,1,0:T(8,128)(2,1)S(1)} %get-tuple-element.678), channel_id=1, source_target_pairs={{0,4},{4,8},{8,12},{12,0},{1,5},{5,9},{9,13},{13,1},{2,6},{6,10},{... | collective-permute-start | bytes 129032 | tf_op jit(solution)/shard_map/ppermute | solution.py:17
  15.3 4.6 %collective-permute-start.1 = (bf16[6,7,512]{2,1,0:T(8,128)(2,1)S(1)}, bf16[6,7,512]{2,1,0:T(8,128)(2,1)S(1)}, u32[]{:S(2)}, u32[]{:S(2)}) collective-permute-start(bf16[6,7,512]{2,1,0:T(8,128)(2,1)S(1)} %get-tuple-element.679), channel_id=1, source_target_pairs={{4,0},{8,4},{12,8},{0,12},{5,1},{9,5},{13,9},{1,13},{6,2},{10,6},{... | collective-permute-start | bytes 129032 | tf_op jit(solution)/shard_map/ppermute | solution.py:18
  20.1 1.3 collective-permute-start.2
  20.2 1.4 collective-permute-start.3
  35.9 0.6 copy-start
  35.9 36.6 %copy-start.4 = (f32[3,32,512]{2,1,0:T(8,128)S(1)}, f32[3,32,512]{2,1,0:T(8,128)}, u32[]{:S(2)}) copy-start(f32[3,32,512]{2,1,0:T(8,128)} %param.17) | copy-start | bytes 589828
  36.5 106.0 %all-reduce.9.cloned.1.call-start = ((), (), s32[]{:S(2)}) async-start(), calls=%async_computation.1 | async-start | bytes 131072 | tf_op jit(solution)/shard_map/psum | solution.py:123
  59.5 4.6 %collective-permute-start.4 = (f32[1,512]{1,0:T(1,128)S(1)}, f32[1,512]{1,0:T(1,128)S(1)}, u32[]{:S(2)}, u32[]{:S(2)}) collective-permute-start(f32[1,512]{1,0:T(1,128)S(1)} %get-tuple-element.693), channel_id=1, source_target_pairs={{4,0},{8,4},{12,8},{0,12},{5,1},{9,5},{13,9},{1,13},{6,2},{10,6},{... | collective-permute-start | bytes 6152 | tf_op jit(solution)/shard_map/ppermute | solution.py:18
  62.8 5.4 %collective-permute-start.5 = (f32[1,512]{1,0:T(1,128)S(1)}, f32[1,512]{1,0:T(1,128)S(1)}, u32[]{:S(2)}, u32[]{:S(2)}) collective-permute-start(f32[1,512]{1,0:T(1,128)S(1)} %get-tuple-element.692), channel_id=1, source_target_pairs={{0,4},{4,8},{8,12},{12,0},{1,5},{5,9},{9,13},{13,1},{2,6},{6,10},{... | collective-permute-start | bytes 6152 | tf_op jit(solution)/shard_map/ppermute | solution.py:17
  69.0 1.2 collective-permute-start.6
  69.1 1.3 collective-permute-start.7
  72.6 5.5 %collective-permute-start.8 = (f32[3,1,512]{2,1,0:T(1,128)S(1)}, f32[3,1,512]{2,1,0:T(1,128)S(1)}, u32[]{:S(2)}, u32[]{:S(2)}) collective-permute-start(f32[3,1,512]{2,1,0:T(1,128)S(1)} %get-tuple-element.676), channel_id=1, source_target_pairs={{0,4},{4,8},{8,12},{12,0},{1,5},{5,9},{9,13},{13,1},{2,6},{6,10},{... | collective-permute-start | bytes 18440 | tf_op jit(solution)/shard_map/ppermute | solution.py:17
  72.6 5.4 %collective-permute-start.9 = (f32[3,1,512]{2,1,0:T(1,128)S(1)}, f32[3,1,512]{2,1,0:T(1,128)S(1)}, u32[]{:S(2)}, u32[]{:S(2)}) collective-permute-start(f32[3,1,512]{2,1,0:T(1,128)S(1)} %get-tuple-element.677), channel_id=1, source_target_pairs={{4,0},{8,4},{12,8},{0,12},{5,1},{9,5},{13,9},{1,13},{6,2},{10,6},{... | collective-permute-start | bytes 18440 | tf_op jit(solution)/shard_map/ppermute | solution.py:18
  78.2 1.3 collective-permute-start.10
  78.2 1.4 collective-permute-start.11
  80.1 5.5 %collective-permute-start.12 = (bf16[7,512]{1,0:T(8,128)(2,1)S(1)}, bf16[7,512]{1,0:T(8,128)(2,1)S(1)}, u32[]{:S(2)}, u32[]{:S(2)}) collective-permute-start(bf16[7,512]{1,0:T(8,128)(2,1)S(1)} %get-tuple-element.760), channel_id=1, source_target_pairs={{0,4},{4,8},{8,12},{12,0},{1,5},{5,9},{9,13},{13,1},{2,6},{6,10},{... | collective-permute-start | bytes 21512 | tf_op jit(solution)/shard_map/ppermute | solution.py:17
  80.1 5.5 %collective-permute-start.13 = (bf16[7,512]{1,0:T(8,128)(2,1)S(1)}, bf16[7,512]{1,0:T(8,128)(2,1)S(1)}, u32[]{:S(2)}, u32[]{:S(2)}) collective-permute-start(bf16[7,512]{1,0:T(8,128)(2,1)S(1)} %get-tuple-element.761), channel_id=1, source_target_pairs={{4,0},{8,4},{12,8},{0,12},{5,1},{9,5},{13,9},{1,13},{6,2},{10,6},{... | collective-permute-start | bytes 21512 | tf_op jit(solution)/shard_map/ppermute | solution.py:18
  85.7 1.2 collective-permute-start.14
  85.7 1.3 collective-permute-start.15
  88.1 7.6 %copy-start.2 = (s32[6,32,512]{2,1,0:T(8,128)S(1)}, s32[6,32,512]{2,1,0:T(8,128)}, u32[]{:S(2)}) copy-start(s32[6,32,512]{2,1,0:T(8,128)} %param.13) | copy-start | bytes 1179652
  88.1 7.6 %copy-start.3 = (bf16[6,32,512]{2,1,0:T(8,128)(2,1)S(1)}, bf16[6,32,512]{2,1,0:T(8,128)(2,1)}, u32[]{:S(2)}) copy-start(bf16[6,32,512]{2,1,0:T(8,128)(2,1)} %param.14) | copy-start | bytes 589828
  98.3 6.3 %collective-permute-start.16 = (bf16[6,7,512]{2,1,0:T(8,128)(2,1)S(1)}, bf16[6,7,512]{2,1,0:T(8,128)(2,1)S(1)}, u32[]{:S(2)}, u32[]{:S(2)}) collective-permute-start(bf16[6,7,512]{2,1,0:T(8,128)(2,1)S(1)} %get-tuple-element.674), channel_id=1, source_target_pairs={{0,4},{4,8},{8,12},{12,0},{1,5},{5,9},{9,13},{13,1},{2,6},{6,10},{... | collective-permute-start | bytes 129032 | tf_op jit(solution)/shard_map/ppermute | solution.py:17
  99.5 5.1 %collective-permute-start.17 = (bf16[6,7,512]{2,1,0:T(8,128)(2,1)S(1)}, bf16[6,7,512]{2,1,0:T(8,128)(2,1)S(1)}, u32[]{:S(2)}, u32[]{:S(2)}) collective-permute-start(bf16[6,7,512]{2,1,0:T(8,128)(2,1)S(1)} %get-tuple-element.675), channel_id=1, source_target_pairs={{4,0},{8,4},{12,8},{0,12},{5,1},{9,5},{13,9},{1,13},{6,2},{10,6},{... | collective-permute-start | bytes 129032 | tf_op jit(solution)/shard_map/ppermute | solution.py:18
  104.7 1.3 collective-permute-start.18
  104.8 1.4 collective-permute-start.19
  120.5 0.6 copy-start.1
  143.2 4.6 %collective-permute-start.20 = (f32[1,512]{1,0:T(1,128)S(1)}, f32[1,512]{1,0:T(1,128)S(1)}, u32[]{:S(2)}, u32[]{:S(2)}) collective-permute-start(f32[1,512]{1,0:T(1,128)S(1)} %get-tuple-element.690), channel_id=1, source_target_pairs={{4,0},{8,4},{12,8},{0,12},{5,1},{9,5},{13,9},{1,13},{6,2},{10,6},{... | collective-permute-start | bytes 6152 | tf_op jit(solution)/shard_map/ppermute | solution.py:18
  146.6 5.4 %collective-permute-start.21 = (f32[1,512]{1,0:T(1,128)S(1)}, f32[1,512]{1,0:T(1,128)S(1)}, u32[]{:S(2)}, u32[]{:S(2)}) collective-permute-start(f32[1,512]{1,0:T(1,128)S(1)} %get-tuple-element.689), channel_id=1, source_target_pairs={{0,4},{4,8},{8,12},{12,0},{1,5},{5,9},{9,13},{13,1},{2,6},{6,10},{... | collective-permute-start | bytes 6152 | tf_op jit(solution)/shard_map/ppermute | solution.py:17
  152.7 1.2 collective-permute-start.22
  152.8 1.3 collective-permute-start.23
  156.3 5.5 %collective-permute-start.24 = (f32[3,1,512]{2,1,0:T(1,128)S(1)}, f32[3,1,512]{2,1,0:T(1,128)S(1)}, u32[]{:S(2)}, u32[]{:S(2)}) collective-permute-start(f32[3,1,512]{2,1,0:T(1,128)S(1)} %get-tuple-element.672), channel_id=1, source_target_pairs={{0,4},{4,8},{8,12},{12,0},{1,5},{5,9},{9,13},{13,1},{2,6},{6,10},{... | collective-permute-start | bytes 18440 | tf_op jit(solution)/shard_map/ppermute | solution.py:17
  156.3 5.4 %collective-permute-start.25 = (f32[3,1,512]{2,1,0:T(1,128)S(1)}, f32[3,1,512]{2,1,0:T(1,128)S(1)}, u32[]{:S(2)}, u32[]{:S(2)}) collective-permute-start(f32[3,1,512]{2,1,0:T(1,128)S(1)} %get-tuple-element.673), channel_id=1, source_target_pairs={{4,0},{8,4},{12,8},{0,12},{5,1},{9,5},{13,9},{1,13},{6,2},{10,6},{... | collective-permute-start | bytes 18440 | tf_op jit(solution)/shard_map/ppermute | solution.py:18
  161.9 1.3 collective-permute-start.26
  161.9 1.4 collective-permute-start.27
  163.8 5.5 %collective-permute-start.28 = (bf16[7,512]{1,0:T(8,128)(2,1)S(1)}, bf16[7,512]{1,0:T(8,128)(2,1)S(1)}, u32[]{:S(2)}, u32[]{:S(2)}) collective-permute-start(bf16[7,512]{1,0:T(8,128)(2,1)S(1)} %get-tuple-element.758), channel_id=1, source_target_pairs={{0,4},{4,8},{8,12},{12,0},{1,5},{5,9},{9,13},{13,1},{2,6},{6,10},{... | collective-permute-start | bytes 21512 | tf_op jit(solution)/shard_map/ppermute | solution.py:17
  163.8 5.5 %collective-permute-start.29 = (bf16[7,512]{1,0:T(8,128)(2,1)S(1)}, bf16[7,512]{1,0:T(8,128)(2,1)S(1)}, u32[]{:S(2)}, u32[]{:S(2)}) collective-permute-start(bf16[7,512]{1,0:T(8,128)(2,1)S(1)} %get-tuple-element.759), channel_id=1, source_target_pairs={{4,0},{8,4},{12,8},{0,12},{5,1},{9,5},{13,9},{1,13},{6,2},{10,6},{... | collective-permute-start | bytes 21512 | tf_op jit(solution)/shard_map/ppermute | solution.py:18
  169.4 1.2 collective-permute-start.30
  169.4 1.3 collective-permute-start.31
  179.4 0.7 copy-start.5
Sparse Core Ops, SparseCore 0:
  36.6 22.0 all-reduce.6
  121.3 21.1 all-reduce.8
where the time goes:
time: 188 us; the launch traced here: 187 us
  waiting for transfers between devices  71.8 us (38%)
  starting transfers between devices  35.8 us (19%)
  local copies, waits for them, and re-layouts  24.8 us (13%)
  matrix products  20.5 us (11%)
  between operations  14.9 us (8%)
  other arithmetic  14.6 us (8%)
  loops' own time  4.55 us (2%)
    psum x2, waiting for transfers between devices, body(): surface = lax.psum(partial_value, 'gz')  43.5 us
    ppermute x16, starting transfers between devices, padded_2(): after = lax.ppermute(initial, axis, down)  29.9 us
    ppermute x16, waiting for transfers between devices, padded_2(): before = lax.ppermute(last, axis, up)  22.8 us
    dot_general x24, matrix products, band_matrices(): jnp.einsum('sc,cpq->spq', kernel, selector, preferred_element_type=jnp.fl...  10.6 us
    dot_general x24, matrix products, banded_sum(): jnp.einsum('rbk,kq->rbq', stacked, weights, preferred_element_type=jnp.fl...  9.84 us
    while x444, local copies, waits for them, and re-layouts  6.95 us
    convert_element_type x24, local copies, waits for them, and re-layouts, band_matrices(): return summed.astype(jnp.bfloat16)  6.3 us
    convert_element_type x2, other arithmetic, body(): rounded = density.astype(jnp.bfloat16)  6.14 us
  transfers between devices with their start and end apart: 34, of which 28 were waited for; matrix products, arithmetic and copies ran while one was open for 0% of the time, Pallas kernels for 0%

commit v1 on v0

--- a/solution.py
+++ b/solution.py
@@ -120,7 +120,7 @@
     for iteration in range(ITERS):
         rounded = density.astype(jnp.bfloat16)
         partial_value = surface_halo(rounded, kernels, selector, block_width, blocks, radius)
-        surface = lax.psum(partial_value, "gz")
+        surface = lax.all_gather(partial_value, "gz").sum(axis=0)
         edged_surface = padded_2(surface, (("gx", 0), ("gy", 1)), 1)
         misfit = jnp.stack(tensor_parts(edged_surface)) - observed
         edged_misfit = padded_2(misfit, (("gx", 1), ("gy", 2)), 1)

time: 188 us -> 133 us (0.71)
  waiting for transfers between devices: 71.8 us -> 28.2 us
  between operations: 14.9 us -> 1.52 us
  blocking collectives: 0 us -> 10.2 us
  other arithmetic: 14.6 us -> 9.72 us
  local copies, waits for them, and re-layouts: 24.8 us -> 22.1 us
    psum x2 -> x0, waiting for transfers between devices: 43.5 us -> none  [body(): surface = lax.psum(partial_value, 'gz')]
    all_gather x0 -> x2, blocking collectives: none -> 10.2 us  [body(): surface = lax.all_gather(partial_value, 'gz').sum(axis=0)]
    another operation x2, other arithmetic: 2.15 us -> 0.24 us  [body(): misfit = jnp.stack(tensor_parts(edged_surface)) - observed]
  transfers between devices with their start and end apart: 34 -> 32, of which waited for: 28 -> 26; matrix products, arithmetic and copies ran while one was open for 0% -> 1% of each run, Pallas kernels for 0% -> 0%
where the time goes in v1:
time: 133 us
  starting transfers between devices  36.1 us (27%)
  waiting for transfers between devices  28.2 us (21%)
  local copies, waits for them, and re-layouts  22.1 us (17%)
  matrix products  20.5 us (15%)
  blocking collectives  10.2 us (8%)
  other arithmetic  9.72 us (7%)
  loops' own time  4.56 us (3%)
  between operations  1.52 us (1%)
    ppermute x16, starting transfers between devices, padded_2(): after = lax.ppermute(initial, axis, down)  30.3 us
    ppermute x16, waiting for transfers between devices, padded_2(): before = lax.ppermute(last, axis, up)  22.8 us
    dot_general x24, matrix products, band_matrices(): jnp.einsum('sc,cpq->spq', kernel, selector, preferred_element_type=jnp.fl...  10.6 us
    all_gather x2, blocking collectives, body(): surface = lax.all_gather(partial_value, 'gz').sum(axis=0)  10.2 us
    dot_general x24, matrix products, banded_sum(): jnp.einsum('rbk,kq->rbq', stacked, weights, preferred_element_type=jnp.fl...  9.84 us
    while x444, local copies, waits for them, and re-layouts  6.95 us
    convert_element_type x2, other arithmetic, body(): rounded = density.astype(jnp.bfloat16)  6.44 us
    convert_element_type x24, local copies, waits for them, and re-layouts, band_matrices(): return summed.astype(jnp.bfloat16)  6.3 us
  transfers between devices with their start and end apart: 32, of which 26 were waited for; matrix products, arithmetic and copies ran while one was open for 1% of the time, Pallas kernels for 0%

profile of v1, /device:TPU:0, one launch (start us, length us, event | category | flops | bytes accessed | tf_op | source)
XLA Modules:
  0.0 132.9 jit_solution(14102285746593834437)
XLA Ops:
  0.6 1.5 %fusion.107 = (f32[1]{0:T(128)}, f32[1]{0:T(128)}, f32[1]{0:T(128)}, f32[1]{0:T(128)}) fusion(f32[4]{0:T(128)} %param.15), kind=kLoop, calls=%fused_computation.464 | loop fusion | bytes 32 | tf_op jit(solution)/shard_map/slice | solution.py:117
  2.1 3.7 %fusion.98 = bf16[6,32,512]{2,1,0:T(8,128)(2,1)S(1)} fusion(f32[]{:T(128)} %bitcast.3, s32[6,32,512]{2,1,0:T(8,128)} %param.13, f32[]{:T(128)} %bitcast.2, f32[]{:T(128)} %bitcast.1, f32[]{:T(128)} %bitcast, bf16[6,32,512]{2,1,0:T(8,128)(2,1)} %param.14), kind=kLoop, calls=%fused_computation.448 | loop fusion | flops 1376256 | bytes 786448 | tf_op jit(solution)/shard_map/convert_element_type | solution.py:121
  5.8 3.1 %collective-permute-start = (bf16[6,7,512]{2,1,0:T(8,128)(2,1)S(1)}, bf16[6,7,512]{2,1,0:T(8,128)(2,1)S(1)}, u32[]{:S(2)}, u32[]{:S(2)}) collective-permute-start(bf16[6,7,512]{2,1,0:T(8,128)(2,1)S(1)} %get-tuple-element.678), channel_id=1, source_target_pairs={{0,4},{4,8},{8,12},{12,0},{1,5},{5,9},{9,13},{13,1},{2,6},{6,10},{... | collective-permute-start | bytes 129032 | tf_op jit(solution)/shard_map/ppermute | solution.py:17
  8.9 2.1 %collective-permute-start.1 = (bf16[6,7,512]{2,1,0:T(8,128)(2,1)S(1)}, bf16[6,7,512]{2,1,0:T(8,128)(2,1)S(1)}, u32[]{:S(2)}, u32[]{:S(2)}) collective-permute-start(bf16[6,7,512]{2,1,0:T(8,128)(2,1)S(1)} %get-tuple-element.679), channel_id=1, source_target_pairs={{4,0},{8,4},{12,8},{0,12},{5,1},{9,5},{13,9},{1,13},{6,2},{10,6},{... | collective-permute-start | bytes 129032 | tf_op jit(solution)/shard_map/ppermute | solution.py:18
  11.0 2.1 %collective-permute-done = bf16[6,7,512]{2,1,0:T(8,128)(2,1)S(1)} collective-permute-done((bf16[6,7,512]{2,1,0:T(8,128)(2,1)S(1)}, bf16[6,7,512]{2,1,0:T(8,128)(2,1)S(1)}, u32[]{:S(2)}, u32[]{:S(2)}) %collective-permute-start) | collective-permute-done | bytes 43040 | tf_op jit(solution)/shard_map/ppermute | solution.py:17
  13.8 0.5 collective-permute-start.3
  14.3 0.8 collective-permute-done.2
  15.5 13.9 %while.62 = (s32[]{:T(128)}, f32[32,512]{1,0:T(8,128)S(1)}, bf16[6,46,640]{2,1,0:T(8,128)(2,1)S(1)}, bf16[6,15,15]{2,1,0:T(8,128)(2,1)S(1)}, s32[]{:T(128)}, /*i...) while((s32[]{:T(128)}, f32[32,512]{1,0:T(8,128)S(1)}, ...), condition=%wide.region_1.2_spmd.clone, body=%wide.region_0.1_spmd.clone.sunk | while | flops 143065104 | bytes 10342823 | solution.py:64
  16.7 0.4 convolution_convert_fusion.10
  19.0 0.4 convolution_convert_fusion.10
  21.3 0.4 convolution_convert_fusion.10
  23.6 0.4 convolution_convert_fusion.10
  26.0 0.4 convolution_convert_fusion.10
  28.3 0.4 convolution_convert_fusion.10
  29.5 5.1 %all-gather = f32[64,512]{1,0:T(8,128)S(1)} all-gather(f32[32,512]{1,0:T(8,128)S(1)} %get-tuple-element.446), channel_id=2, replica_groups=mesh['runs'=2,'gx'=4,'gy'=2,'gz'=2] {'gz'}, dimensions={0}, use_global_device_ids=true | all-gather | bytes 196608 | tf_op jit(solution)/shard_map/all_gather | solution.py:123
  34.6 3.4 %collective-permute-start.4 = (f32[1,512]{1,0:T(1,128)S(1)}, f32[1,512]{1,0:T(1,128)S(1)}, u32[]{:S(2)}, u32[]{:S(2)}) collective-permute-start(f32[1,512]{1,0:T(1,128)S(1)} %get-tuple-element.693), channel_id=1, source_target_pairs={{4,0},{8,4},{12,8},{0,12},{5,1},{9,5},{13,9},{1,13},{6,2},{10,6},{... | collective-permute-start | bytes 6152 | tf_op jit(solution)/shard_map/ppermute | solution.py:18
  38.0 1.3 collective-permute-done.4
  39.4 4.1 %collective-permute-done.5 = f32[1,512]{1,0:T(1,128)S(1)} collective-permute-done((f32[1,512]{1,0:T(1,128)S(1)}, f32[1,512]{1,0:T(1,128)S(1)}, u32[]{:S(2)}, u32[]{:S(2)}) %collective-permute-start.5) | collective-permute-done | bytes 2080 | tf_op jit(solution)/shard_map/ppermute | solution.py:17
  43.5 0.5 collective-permute-start.7
  44.0 0.7 collective-permute-done.6
  45.2 3.8 %collective-permute-start.9 = (f32[3,1,512]{2,1,0:T(1,128)S(1)}, f32[3,1,512]{2,1,0:T(1,128)S(1)}, u32[]{:S(2)}, u32[]{:S(2)}) collective-permute-start(f32[3,1,512]{2,1,0:T(1,128)S(1)} %get-tuple-element.677), channel_id=1, source_target_pairs={{4,0},{8,4},{12,8},{0,12},{5,1},{9,5},{13,9},{1,13},{6,2},{10,6},{... | collective-permute-start | bytes 18440 | tf_op jit(solution)/shard_map/ppermute | solution.py:18
  49.1 1.6 %collective-permute-done.8 = f32[3,1,512]{2,1,0:T(1,128)S(1)} collective-permute-done((f32[3,1,512]{2,1,0:T(1,128)S(1)}, f32[3,1,512]{2,1,0:T(1,128)S(1)}, u32[]{:S(2)}, u32[]{:S(2)}) %collective-permute-start.8) | collective-permute-done | bytes 6176 | tf_op jit(solution)/shard_map/ppermute | solution.py:17
  50.8 0.5 collective-permute-start.11
  51.3 0.7 collective-permute-done.10
  52.7 3.9 %collective-permute-start.13 = (bf16[7,512]{1,0:T(8,128)(2,1)S(1)}, bf16[7,512]{1,0:T(8,128)(2,1)S(1)}, u32[]{:S(2)}, u32[]{:S(2)}) collective-permute-start(bf16[7,512]{1,0:T(8,128)(2,1)S(1)} %get-tuple-element.761), channel_id=1, source_target_pairs={{4,0},{8,4},{12,8},{0,12},{5,1},{9,5},{13,9},{1,13},{6,2},{10,6},{... | collective-permute-start | bytes 21512 | tf_op jit(solution)/shard_map/ppermute | solution.py:18
  56.6 1.6 %collective-permute-done.12 = bf16[7,512]{1,0:T(8,128)(2,1)S(1)} collective-permute-done((bf16[7,512]{1,0:T(8,128)(2,1)S(1)}, bf16[7,512]{1,0:T(8,128)(2,1)S(1)}, u32[]{:S(2)}, u32[]{:S(2)}) %collective-permute-start.12) | collective-permute-done | bytes 7200 | tf_op jit(solution)/shard_map/ppermute | solution.py:17
  58.3 0.5 collective-permute-start.15
  58.9 0.6 collective-permute-done.14
  60.7 7.6 %while.60 = (s32[]{:T(128)}, f32[6,32,512]{2,1,0:T(8,128)S(1)}, bf16[6,15,15]{2,1,0:T(8,128)(2,1)S(1)}, bf16[32,4,3840]{2,0,1:T(8,128)(2,1)S(1)}, s32[]{:T(128)}) while((s32[]{:T(128)}, f32[6,32,512]{2,1,0:T(8,128)S(1)}, bf16[6,15,15]{2,1,0:T(8,128)(2,1)S(1)}, bf16[32,4,3840]{2,0,1:T(8,128)(2,1)S(1)}, s32[]{:T(128)}) %tuple.339), condition=%wide.region_4.5_spmd.clone, body=%wide.region_3.4_spmd.clone.sunk | while | flops 143032320 | bytes 5378117 | solution.py:101
  63.3 0.4 convolution_convert_fusion.8
  65.8 0.4 convolution_convert_fusion.8
  68.3 2.7 %subtract_convert_fusion = bf16[6,32,512]{2,1,0:T(8,128)(2,1)S(1)} fusion(f32[6,32,512]{2,1,0:T(8,128)S(1)} %get-tuple-element.447, f32[]{:T(128)} %bitcast.3, s32[6,32,512]{2,1,0:T(8,128)S(1)} %copy-done, f32[]{:T(128)} %bitcast.2, f32[]{:T(128)} %bitcast.1, f32[]{:T(128)} %bitcast, bf16[6,32,512]{2,1,0:T(8,128)(2,1)S(1)} %copy-done.1), kind=kLoop, calls=%fused_computation.213 | loop fusion | flops 1572864 | bytes 1179664 | tf_op jit(solution)/shard_map/convert_element_type | solution.py:121
  71.1 1.1 collective-permute-start.16
  72.2 2.8 %collective-permute-start.17 = (bf16[6,7,512]{2,1,0:T(8,128)(2,1)S(1)}, bf16[6,7,512]{2,1,0:T(8,128)(2,1)S(1)}, u32[]{:S(2)}, u32[]{:S(2)}) collective-permute-start(bf16[6,7,512]{2,1,0:T(8,128)(2,1)S(1)} %get-tuple-element.675), channel_id=1, source_target_pairs={{4,0},{8,4},{12,8},{0,12},{5,1},{9,5},{13,9},{1,13},{6,2},{10,6},{... | collective-permute-start | bytes 129032 | tf_op jit(solution)/shard_map/ppermute | solution.py:18
  75.0 2.3 %collective-permute-done.16 = bf16[6,7,512]{2,1,0:T(8,128)(2,1)S(1)} collective-permute-done((bf16[6,7,512]{2,1,0:T(8,128)(2,1)S(1)}, bf16[6,7,512]{2,1,0:T(8,128)(2,1)S(1)}, u32[]{:S(2)}, u32[]{:S(2)}) %collective-permute-start.16) | collective-permute-done | bytes 43040 | tf_op jit(solution)/shard_map/ppermute | solution.py:17
  77.6 0.5 collective-permute-start.19
  78.1 0.8 collective-permute-done.18
  79.3 13.9 %while.63 = (s32[]{:T(128)}, f32[32,512]{1,0:T(8,128)S(1)}, bf16[6,46,640]{2,1,0:T(8,128)(2,1)S(1)}, bf16[6,15,15]{2,1,0:T(8,128)(2,1)S(1)}, s32[]{:T(128)}, /*i...) while((s32[]{:T(128)}, f32[32,512]{1,0:T(8,128)S(1)}, ...), condition=%wide.region_6.7_spmd.clone, body=%wide.region_5.6_spmd.clone.sunk | while | flops 143065104 | bytes 10342823 | solution.py:64
  80.4 0.4 convolution_convert_fusion.11
  82.8 0.4 convolution_convert_fusion.11
  85.1 0.4 convolution_convert_fusion.11
  87.4 0.4 convolution_convert_fusion.11
  89.7 0.4 convolution_convert_fusion.11
  92.1 0.4 convolution_convert_fusion.11
  93.2 5.0 %all-gather.1 = f32[64,512]{1,0:T(8,128)S(1)} all-gather(f32[32,512]{1,0:T(8,128)S(1)} %get-tuple-element.448), channel_id=3, replica_groups=mesh['runs'=2,'gx'=4,'gy'=2,'gz'=2] {'gz'}, dimensions={0}, use_global_device_ids=true | all-gather | bytes 196608 | tf_op jit(solution)/shard_map/all_gather | solution.py:123
  98.3 3.6 %collective-permute-start.20 = (f32[1,512]{1,0:T(1,128)S(1)}, f32[1,512]{1,0:T(1,128)S(1)}, u32[]{:S(2)}, u32[]{:S(2)}) collective-permute-start(f32[1,512]{1,0:T(1,128)S(1)} %get-tuple-element.690), channel_id=1, source_target_pairs={{4,0},{8,4},{12,8},{0,12},{5,1},{9,5},{13,9},{1,13},{6,2},{10,6},{... | collective-permute-start | bytes 6152 | tf_op jit(solution)/shard_map/ppermute | solution.py:18
  101.9 1.3 collective-permute-done.20
  103.2 4.1 %collective-permute-done.21 = f32[1,512]{1,0:T(1,128)S(1)} collective-permute-done((f32[1,512]{1,0:T(1,128)S(1)}, f32[1,512]{1,0:T(1,128)S(1)}, u32[]{:S(2)}, u32[]{:S(2)}) %collective-permute-start.21) | collective-permute-done | bytes 2080 | tf_op jit(solution)/shard_map/ppermute | solution.py:17
  107.4 0.5 collective-permute-start.23
  107.9 0.7 collective-permute-done.22
  109.1 3.8 %collective-permute-start.25 = (f32[3,1,512]{2,1,0:T(1,128)S(1)}, f32[3,1,512]{2,1,0:T(1,128)S(1)}, u32[]{:S(2)}, u32[]{:S(2)}) collective-permute-start(f32[3,1,512]{2,1,0:T(1,128)S(1)} %get-tuple-element.673), channel_id=1, source_target_pairs={{4,0},{8,4},{12,8},{0,12},{5,1},{9,5},{13,9},{1,13},{6,2},{10,6},{... | collective-permute-start | bytes 18440 | tf_op jit(solution)/shard_map/ppermute | solution.py:18
  112.9 1.6 %collective-permute-done.24 = f32[3,1,512]{2,1,0:T(1,128)S(1)} collective-permute-done((f32[3,1,512]{2,1,0:T(1,128)S(1)}, f32[3,1,512]{2,1,0:T(1,128)S(1)}, u32[]{:S(2)}, u32[]{:S(2)}) %collective-permute-start.24) | collective-permute-done | bytes 6176 | tf_op jit(solution)/shard_map/ppermute | solution.py:17
  114.7 0.5 collective-permute-start.27
  115.2 0.7 collective-permute-done.26
  116.6 3.9 %collective-permute-start.29 = (bf16[7,512]{1,0:T(8,128)(2,1)S(1)}, bf16[7,512]{1,0:T(8,128)(2,1)S(1)}, u32[]{:S(2)}, u32[]{:S(2)}) collective-permute-start(bf16[7,512]{1,0:T(8,128)(2,1)S(1)} %get-tuple-element.759), channel_id=1, source_target_pairs={{4,0},{8,4},{12,8},{0,12},{5,1},{9,5},{13,9},{1,13},{6,2},{10,6},{... | collective-permute-start | bytes 21512 | tf_op jit(solution)/shard_map/ppermute | solution.py:18
  120.5 1.6 %collective-permute-done.28 = bf16[7,512]{1,0:T(8,128)(2,1)S(1)} collective-permute-done((bf16[7,512]{1,0:T(8,128)(2,1)S(1)}, bf16[7,512]{1,0:T(8,128)(2,1)S(1)}, u32[]{:S(2)}, u32[]{:S(2)}) %collective-permute-start.28) | collective-permute-done | bytes 7200 | tf_op jit(solution)/shard_map/ppermute | solution.py:17
  122.2 0.5 collective-permute-start.31
  122.7 0.6 constant_dynamic-slice_fusion
  124.6 7.6 %while.61 = (s32[]{:T(128)}, f32[6,32,512]{2,1,0:T(8,128)S(1)}, bf16[6,15,15]{2,1,0:T(8,128)(2,1)S(1)}, bf16[32,4,3840]{2,0,1:T(8,128)(2,1)S(1)}, s32[]{:T(128)}) while((s32[]{:T(128)}, f32[6,32,512]{2,1,0:T(8,128)S(1)}, bf16[6,15,15]{2,1,0:T(8,128)(2,1)S(1)}, bf16[32,4,3840]{2,0,1:T(8,128)(2,1)S(1)}, s32[]{:T(128)}) %tuple.350), condition=%wide.region_9.10_spmd.clone, body=%wide.region_8.9_spmd.clone.sunk | while | flops 143032320 | bytes 5378117 | solution.py:101
  124.6 0.4 convolution_convert_fusion.9
  125.9 0.4 convolution_convert_fusion.9
  128.4 0.4 convolution_convert_fusion.9
  130.9 0.4 convolution_convert_fusion.9
  132.2 0.7 copy-done.3
  (713 shorter events, 37.4 us)
Async XLA Ops:
  2.1 13.4 %copy-start.4 = (bf16[6,15,15]{2,1,0:T(8,128)(2,1)S(1)}, bf16[6,15,15]{2,1,0:T(8,128)(2,1)}, u32[]{:S(2)}) copy-start(bf16[6,15,15]{2,1,0:T(8,128)(2,1)} %param.16) | copy-start | bytes 8104
  5.8 7.3 %collective-permute-start = (bf16[6,7,512]{2,1,0:T(8,128)(2,1)S(1)}, bf16[6,7,512]{2,1,0:T(8,128)(2,1)S(1)}, u32[]{:S(2)}, u32[]{:S(2)}) collective-permute-start(bf16[6,7,512]{2,1,0:T(8,128)(2,1)S(1)} %get-tuple-element.678), channel_id=1, source_target_pairs={{0,4},{4,8},{8,12},{12,0},{1,5},{5,9},{9,13},{13,1},{2,6},{6,10},{... | collective-permute-start | bytes 129032 | tf_op jit(solution)/shard_map/ppermute | solution.py:17
  8.9 4.6 %collective-permute-start.1 = (bf16[6,7,512]{2,1,0:T(8,128)(2,1)S(1)}, bf16[6,7,512]{2,1,0:T(8,128)(2,1)S(1)}, u32[]{:S(2)}, u32[]{:S(2)}) collective-permute-start(bf16[6,7,512]{2,1,0:T(8,128)(2,1)S(1)} %get-tuple-element.679), channel_id=1, source_target_pairs={{4,0},{8,4},{12,8},{0,12},{5,1},{9,5},{13,9},{1,13},{6,2},{10,6},{... | collective-permute-start | bytes 129032 | tf_op jit(solution)/shard_map/ppermute | solution.py:18
  13.7 1.3 %collective-permute-start.2 = (bf16[6,46,7]{2,1,0:T(8,128)(2,1)S(1)}, bf16[6,46,7]{2,1,0:T(8,128)(2,1)S(1)}, u32[]{:S(2)}, u32[]{:S(2)}) collective-permute-start(bf16[6,46,7]{2,1,0:T(8,128)(2,1)S(1)} %get-tuple-element.662), channel_id=1, source_target_pairs={{0,2},{2,0},{1,3},{3,1},{4,6},{6,4},{5,7},{7,5},{8,10},{10,8},{9,1... | collective-permute-start | bytes 11600 | tf_op jit(solution)/shard_map/ppermute | solution.py:17
  13.8 1.4 %collective-permute-start.3 = (bf16[6,46,7]{2,1,0:T(8,128)(2,1)S(1)}, bf16[6,46,7]{2,1,0:T(8,128)(2,1)S(1)}, u32[]{:S(2)}, u32[]{:S(2)}) collective-permute-start(bf16[6,46,7]{2,1,0:T(8,128)(2,1)S(1)} %get-tuple-element.663), channel_id=1, source_target_pairs={{2,0},{0,2},{3,1},{1,3},{6,4},{4,6},{7,5},{5,7},{10,8},{8,10},{11,... | collective-permute-start | bytes 11600 | tf_op jit(solution)/shard_map/ppermute | solution.py:18
  29.5 15.7 %copy-start.2 = (f32[3,32,512]{2,1,0:T(8,128)S(1)}, f32[3,32,512]{2,1,0:T(8,128)}, u32[]{:S(2)}) copy-start(f32[3,32,512]{2,1,0:T(8,128)} %param.17) | copy-start | bytes 589828
  34.6 4.7 %collective-permute-start.4 = (f32[1,512]{1,0:T(1,128)S(1)}, f32[1,512]{1,0:T(1,128)S(1)}, u32[]{:S(2)}, u32[]{:S(2)}) collective-permute-start(f32[1,512]{1,0:T(1,128)S(1)} %get-tuple-element.693), channel_id=1, source_target_pairs={{4,0},{8,4},{12,8},{0,12},{5,1},{9,5},{13,9},{1,13},{6,2},{10,6},{... | collective-permute-start | bytes 6152 | tf_op jit(solution)/shard_map/ppermute | solution.py:18
  38.0 5.4 %collective-permute-start.5 = (f32[1,512]{1,0:T(1,128)S(1)}, f32[1,512]{1,0:T(1,128)S(1)}, u32[]{:S(2)}, u32[]{:S(2)}) collective-permute-start(f32[1,512]{1,0:T(1,128)S(1)} %get-tuple-element.692), channel_id=1, source_target_pairs={{0,4},{4,8},{8,12},{12,0},{1,5},{5,9},{9,13},{13,1},{2,6},{6,10},{... | collective-permute-start | bytes 6152 | tf_op jit(solution)/shard_map/ppermute | solution.py:17
  43.5 1.2 collective-permute-start.6
  43.5 1.3 %collective-permute-start.7 = (f32[34,1]{1,0:T(8,128)S(1)}, f32[34,1]{1,0:T(8,128)S(1)}, u32[]{:S(2)}, u32[]{:S(2)}) collective-permute-start(f32[34,1]{1,0:T(8,128)S(1)} %get-tuple-element.687), channel_id=1, source_target_pairs={{0,2},{2,0},{1,3},{3,1},{4,6},{6,4},{5,7},{7,5},{8,10},{10,8},{9,1... | collective-permute-start | bytes 416 | tf_op jit(solution)/shard_map/ppermute | solution.py:17
  45.2 5.5 %collective-permute-start.8 = (f32[3,1,512]{2,1,0:T(1,128)S(1)}, f32[3,1,512]{2,1,0:T(1,128)S(1)}, u32[]{:S(2)}, u32[]{:S(2)}) collective-permute-start(f32[3,1,512]{2,1,0:T(1,128)S(1)} %get-tuple-element.676), channel_id=1, source_target_pairs={{0,4},{4,8},{8,12},{12,0},{1,5},{5,9},{9,13},{13,1},{2,6},{6,10},{... | collective-permute-start | bytes 18440 | tf_op jit(solution)/shard_map/ppermute | solution.py:17
  45.2 5.4 %collective-permute-start.9 = (f32[3,1,512]{2,1,0:T(1,128)S(1)}, f32[3,1,512]{2,1,0:T(1,128)S(1)}, u32[]{:S(2)}, u32[]{:S(2)}) collective-permute-start(f32[3,1,512]{2,1,0:T(1,128)S(1)} %get-tuple-element.677), channel_id=1, source_target_pairs={{4,0},{8,4},{12,8},{0,12},{5,1},{9,5},{13,9},{1,13},{6,2},{10,6},{... | collective-permute-start | bytes 18440 | tf_op jit(solution)/shard_map/ppermute | solution.py:18
  50.8 1.3 collective-permute-start.10
  50.8 1.4 %collective-permute-start.11 = (f32[3,34,1]{2,1,0:T(8,128)S(1)}, f32[3,34,1]{2,1,0:T(8,128)S(1)}, u32[]{:S(2)}, u32[]{:S(2)}) collective-permute-start(f32[3,34,1]{2,1,0:T(8,128)S(1)} %get-tuple-element.667), channel_id=1, source_target_pairs={{2,0},{0,2},{3,1},{1,3},{6,4},{4,6},{7,5},{5,7},{10,8},{8,10},{11,... | collective-permute-start | bytes 1232 | tf_op jit(solution)/shard_map/ppermute | solution.py:18
  52.7 5.5 %collective-permute-start.12 = (bf16[7,512]{1,0:T(8,128)(2,1)S(1)}, bf16[7,512]{1,0:T(8,128)(2,1)S(1)}, u32[]{:S(2)}, u32[]{:S(2)}) collective-permute-start(bf16[7,512]{1,0:T(8,128)(2,1)S(1)} %get-tuple-element.760), channel_id=1, source_target_pairs={{0,4},{4,8},{8,12},{12,0},{1,5},{5,9},{9,13},{13,1},{2,6},{6,10},{... | collective-permute-start | bytes 21512 | tf_op jit(solution)/shard_map/ppermute | solution.py:17
  52.7 5.5 %collective-permute-start.13 = (bf16[7,512]{1,0:T(8,128)(2,1)S(1)}, bf16[7,512]{1,0:T(8,128)(2,1)S(1)}, u32[]{:S(2)}, u32[]{:S(2)}) collective-permute-start(bf16[7,512]{1,0:T(8,128)(2,1)S(1)} %get-tuple-element.761), channel_id=1, source_target_pairs={{4,0},{8,4},{12,8},{0,12},{5,1},{9,5},{13,9},{1,13},{6,2},{10,6},{... | collective-permute-start | bytes 21512 | tf_op jit(solution)/shard_map/ppermute | solution.py:18
  58.3 1.2 collective-permute-start.14
  58.3 1.3 %collective-permute-start.15 = (bf16[46,7]{1,0:T(8,128)(2,1)S(1)}, bf16[46,7]{1,0:T(8,128)(2,1)S(1)}, u32[]{:S(2)}, u32[]{:S(2)}) collective-permute-start(bf16[46,7]{1,0:T(8,128)(2,1)S(1)} %get-tuple-element.756), channel_id=1, source_target_pairs={{2,0},{0,2},{3,1},{1,3},{6,4},{4,6},{7,5},{5,7},{10,8},{8,10},{11,... | collective-permute-start | bytes 1940 | tf_op jit(solution)/shard_map/ppermute | solution.py:18
  60.7 7.6 %copy-start = (s32[6,32,512]{2,1,0:T(8,128)S(1)}, s32[6,32,512]{2,1,0:T(8,128)}, u32[]{:S(2)}) copy-start(s32[6,32,512]{2,1,0:T(8,128)} %param.13) | copy-start | bytes 1179652
  60.7 7.6 %copy-start.1 = (bf16[6,32,512]{2,1,0:T(8,128)(2,1)S(1)}, bf16[6,32,512]{2,1,0:T(8,128)(2,1)}, u32[]{:S(2)}) copy-start(bf16[6,32,512]{2,1,0:T(8,128)(2,1)} %param.14) | copy-start | bytes 589828
  71.1 6.3 %collective-permute-start.16 = (bf16[6,7,512]{2,1,0:T(8,128)(2,1)S(1)}, bf16[6,7,512]{2,1,0:T(8,128)(2,1)S(1)}, u32[]{:S(2)}, u32[]{:S(2)}) collective-permute-start(bf16[6,7,512]{2,1,0:T(8,128)(2,1)S(1)} %get-tuple-element.674), channel_id=1, source_target_pairs={{0,4},{4,8},{8,12},{12,0},{1,5},{5,9},{9,13},{13,1},{2,6},{6,10},{... | collective-permute-start | bytes 129032 | tf_op jit(solution)/shard_map/ppermute | solution.py:17
  72.2 5.1 %collective-permute-start.17 = (bf16[6,7,512]{2,1,0:T(8,128)(2,1)S(1)}, bf16[6,7,512]{2,1,0:T(8,128)(2,1)S(1)}, u32[]{:S(2)}, u32[]{:S(2)}) collective-permute-start(bf16[6,7,512]{2,1,0:T(8,128)(2,1)S(1)} %get-tuple-element.675), channel_id=1, source_target_pairs={{4,0},{8,4},{12,8},{0,12},{5,1},{9,5},{13,9},{1,13},{6,2},{10,6},{... | collective-permute-start | bytes 129032 | tf_op jit(solution)/shard_map/ppermute | solution.py:18
  77.5 1.3 %collective-permute-start.18 = (bf16[6,46,7]{2,1,0:T(8,128)(2,1)S(1)}, bf16[6,46,7]{2,1,0:T(8,128)(2,1)S(1)}, u32[]{:S(2)}, u32[]{:S(2)}) collective-permute-start(bf16[6,46,7]{2,1,0:T(8,128)(2,1)S(1)} %get-tuple-element.660), channel_id=1, source_target_pairs={{0,2},{2,0},{1,3},{3,1},{4,6},{6,4},{5,7},{7,5},{8,10},{10,8},{9,1... | collective-permute-start | bytes 11600 | tf_op jit(solution)/shard_map/ppermute | solution.py:17
  77.6 1.4 %collective-permute-start.19 = (bf16[6,46,7]{2,1,0:T(8,128)(2,1)S(1)}, bf16[6,46,7]{2,1,0:T(8,128)(2,1)S(1)}, u32[]{:S(2)}, u32[]{:S(2)}) collective-permute-start(bf16[6,46,7]{2,1,0:T(8,128)(2,1)S(1)} %get-tuple-element.661), channel_id=1, source_target_pairs={{2,0},{0,2},{3,1},{1,3},{6,4},{4,6},{7,5},{5,7},{10,8},{8,10},{11,... | collective-permute-start | bytes 11600 | tf_op jit(solution)/shard_map/ppermute | solution.py:18
  98.3 4.9 %collective-permute-start.20 = (f32[1,512]{1,0:T(1,128)S(1)}, f32[1,512]{1,0:T(1,128)S(1)}, u32[]{:S(2)}, u32[]{:S(2)}) collective-permute-start(f32[1,512]{1,0:T(1,128)S(1)} %get-tuple-element.690), channel_id=1, source_target_pairs={{4,0},{8,4},{12,8},{0,12},{5,1},{9,5},{13,9},{1,13},{6,2},{10,6},{... | collective-permute-start | bytes 6152 | tf_op jit(solution)/shard_map/ppermute | solution.py:18
  101.9 5.4 %collective-permute-start.21 = (f32[1,512]{1,0:T(1,128)S(1)}, f32[1,512]{1,0:T(1,128)S(1)}, u32[]{:S(2)}, u32[]{:S(2)}) collective-permute-start(f32[1,512]{1,0:T(1,128)S(1)} %get-tuple-element.689), channel_id=1, source_target_pairs={{0,4},{4,8},{8,12},{12,0},{1,5},{5,9},{9,13},{13,1},{2,6},{6,10},{... | collective-permute-start | bytes 6152 | tf_op jit(solution)/shard_map/ppermute | solution.py:17
  107.4 1.2 collective-permute-start.22
  107.4 1.3 %collective-permute-start.23 = (f32[34,1]{1,0:T(8,128)S(1)}, f32[34,1]{1,0:T(8,128)S(1)}, u32[]{:S(2)}, u32[]{:S(2)}) collective-permute-start(f32[34,1]{1,0:T(8,128)S(1)} %get-tuple-element.683), channel_id=1, source_target_pairs={{0,2},{2,0},{1,3},{3,1},{4,6},{6,4},{5,7},{7,5},{8,10},{10,8},{9,1... | collective-permute-start | bytes 416 | tf_op jit(solution)/shard_map/ppermute | solution.py:17
  109.0 5.5 %collective-permute-start.24 = (f32[3,1,512]{2,1,0:T(1,128)S(1)}, f32[3,1,512]{2,1,0:T(1,128)S(1)}, u32[]{:S(2)}, u32[]{:S(2)}) collective-permute-start(f32[3,1,512]{2,1,0:T(1,128)S(1)} %get-tuple-element.672), channel_id=1, source_target_pairs={{0,4},{4,8},{8,12},{12,0},{1,5},{5,9},{9,13},{13,1},{2,6},{6,10},{... | collective-permute-start | bytes 18440 | tf_op jit(solution)/shard_map/ppermute | solution.py:17
  109.1 5.4 %collective-permute-start.25 = (f32[3,1,512]{2,1,0:T(1,128)S(1)}, f32[3,1,512]{2,1,0:T(1,128)S(1)}, u32[]{:S(2)}, u32[]{:S(2)}) collective-permute-start(f32[3,1,512]{2,1,0:T(1,128)S(1)} %get-tuple-element.673), channel_id=1, source_target_pairs={{4,0},{8,4},{12,8},{0,12},{5,1},{9,5},{13,9},{1,13},{6,2},{10,6},{... | collective-permute-start | bytes 18440 | tf_op jit(solution)/shard_map/ppermute | solution.py:18
  114.6 1.3 collective-permute-start.26
  114.7 1.4 %collective-permute-start.27 = (f32[3,34,1]{2,1,0:T(8,128)S(1)}, f32[3,34,1]{2,1,0:T(8,128)S(1)}, u32[]{:S(2)}, u32[]{:S(2)}) collective-permute-start(f32[3,34,1]{2,1,0:T(8,128)S(1)} %get-tuple-element.665), channel_id=1, source_target_pairs={{2,0},{0,2},{3,1},{1,3},{6,4},{4,6},{7,5},{5,7},{10,8},{8,10},{11,... | collective-permute-start | bytes 1232 | tf_op jit(solution)/shard_map/ppermute | solution.py:18
  116.5 5.5 %collective-permute-start.28 = (bf16[7,512]{1,0:T(8,128)(2,1)S(1)}, bf16[7,512]{1,0:T(8,128)(2,1)S(1)}, u32[]{:S(2)}, u32[]{:S(2)}) collective-permute-start(bf16[7,512]{1,0:T(8,128)(2,1)S(1)} %get-tuple-element.758), channel_id=1, source_target_pairs={{0,4},{4,8},{8,12},{12,0},{1,5},{5,9},{9,13},{13,1},{2,6},{6,10},{... | collective-permute-start | bytes 21512 | tf_op jit(solution)/shard_map/ppermute | solution.py:17
  116.6 5.5 %collective-permute-start.29 = (bf16[7,512]{1,0:T(8,128)(2,1)S(1)}, bf16[7,512]{1,0:T(8,128)(2,1)S(1)}, u32[]{:S(2)}, u32[]{:S(2)}) collective-permute-start(bf16[7,512]{1,0:T(8,128)(2,1)S(1)} %get-tuple-element.759), channel_id=1, source_target_pairs={{4,0},{8,4},{12,8},{0,12},{5,1},{9,5},{13,9},{1,13},{6,2},{10,6},{... | collective-permute-start | bytes 21512 | tf_op jit(solution)/shard_map/ppermute | solution.py:18
  122.2 1.2 collective-permute-start.30
  122.2 1.3 %collective-permute-start.31 = (bf16[46,7]{1,0:T(8,128)(2,1)S(1)}, bf16[46,7]{1,0:T(8,128)(2,1)S(1)}, u32[]{:S(2)}, u32[]{:S(2)}) collective-permute-start(bf16[46,7]{1,0:T(8,128)(2,1)S(1)} %get-tuple-element.754), channel_id=1, source_target_pairs={{2,0},{0,2},{3,1},{1,3},{6,4},{4,6},{7,5},{5,7},{10,8},{8,10},{11,... | collective-permute-start | bytes 1940 | tf_op jit(solution)/shard_map/ppermute | solution.py:18
  132.1 0.7 copy-start.3
